TPU v7x, 32 devices: a whole 2x2x4 slice. The times are simulated.
32 devices in a mesh: groups: 2 (over x), row: 16 (over z, y, core).
Axes of the slice: x: 2, y: 2, z: 4, core: 2. Of those that a mesh axis runs over, the one named last changes fastest.
Arguments:
- features: bfloat16 [16384, 128], P(('groups', 'row')), parts along dimension 0, may hold values from -6 to 6
- weight: bfloat16 [128, 256], replicated, may hold values from -0.5 to 0.5
- block_cols: int32 [128, 16], P(('groups', 'row')), parts along dimension 0, may hold values from 0 to 63, as said below
- block_counts: int32 [128], P(('groups', 'row')), parts along dimension 0, may hold values from 1 to 16, as said below
- block_vals: bfloat16 [128, 16, 128, 128], P(('groups', 'row')), parts along dimension 0, may hold values from 0 to 0.03125, as said below
- out_grad: bfloat16 [16384, 256], P(('groups', 'row')), parts along dimension 0, may hold values from -6 to 6
Outputs:
- hidden_out: bfloat16 [16384, 256], P(('groups', 'row')), parts along dimension 0
- feat_grad: bfloat16 [16384, 128], P(('groups', 'row')), parts along dimension 0
- weight_grad: float32 [256, 256], P('groups'), parts along dimension 0
There are 2 independent parts, one for each index of `groups`. A program takes and returns all parts, laid end to end along the dimension named above; an argument that names none is the same for every part. Nothing has to cross between parts.
Inputs may be any that keep to these rules, and one draw needn't show every extreme that they name: `block_cols`: within a row panel the first block_counts entries are distinct block columns; entries past the count are valid indices but are not part of A. `block_counts`: some panel holds exactly 16 blocks. `block_vals`: A is symmetric: where panel p stores a block at block column q, panel q stores the transposed block at block column p.
All inputs are finite; a program needn't handle non-finite values.
Results may differ from a plain program's by a relative error of at most 0.005.
Values may be sent and summed in bfloat16 or wider, within the bound.
No kernel may reach another device: no remote copies, remote signals or barrier semaphores. Data moves between devices by JAX's collectives and lax.ppermute only.
A program may use at most 64 MiB of HBM per device.

v0:
```python
import jax
import jax.numpy as jnp
from jax import lax
from jax.sharding import PartitionSpec as P


def body(features, weight, block_cols, block_counts, block_vals, out_grad):
    panel_total, slot_count, block_side, _ = block_vals.shape
    node_rows = features.shape[0]
    in_width = features.shape[1]
    in_use = jnp.arange(slot_count, dtype=jnp.int32)[None, :] < block_counts[:, None]
    blocks = jnp.where(in_use[:, :, None, None], block_vals, jnp.zeros_like(block_vals))
    whole = lax.all_gather(features, "row", axis=0, tiled=True)
    col_blocks = whole.shape[0] // block_side
    picked = whole.reshape(col_blocks, block_side, in_width)[block_cols]
    aggregated = jnp.einsum(
        "pbij,pbjf->pif", blocks, picked, preferred_element_type=jnp.float32
    ).reshape(node_rows, in_width)
    weight_wide = weight.astype(jnp.float32)
    preact = jnp.dot(aggregated, weight_wide, precision=lax.Precision.HIGHEST)
    hidden, pullback = jax.vjp(jax.nn.gelu, preact)
    pre_grad = pullback(out_grad.astype(jnp.float32))[0]
    partial_value = jnp.dot(aggregated.T, pre_grad, precision=lax.Precision.HIGHEST)
    edge_grad = jnp.dot(pre_grad, weight_wide.T, precision=lax.Precision.HIGHEST).astype(
        jnp.bfloat16
    )
    contrib = jnp.einsum(
        "pbij,pif->pbjf",
        blocks,
        edge_grad.reshape(panel_total, block_side, in_width),
        preferred_element_type=jnp.float32,
    )
    contrib = contrib.reshape(panel_total * slot_count, block_side, in_width)
    flat_cols = block_cols.reshape(-1)
    summed = jax.ops.segment_sum(
        contrib, flat_cols, num_segments=lax.axis_size("row") * node_rows // block_side
    )
    feat_term = lax.psum_scatter(
        summed.reshape(lax.axis_size("row") * node_rows, in_width),
        "row",
        scatter_dimension=0,
        tiled=True,
    )
    feat_grad = feat_term.astype(jnp.bfloat16)
    weight_grad = lax.psum(partial_value, "row")
    return (hidden.astype(jnp.bfloat16), feat_grad, weight_grad)


def solution(mesh):
    in_specs = (
        P(("groups", "row"), None),
        P(),
        P(("groups", "row"), None),
        P(("groups", "row")),
        P(("groups", "row"), None, None, None),
        P(("groups", "row"), None),
    )
    out_specs = (P(("groups", "row"), None), P(("groups", "row"), None), P("groups", None))
    return jax.shard_map(body, mesh=mesh, in_specs=in_specs, out_specs=out_specs, check_vma=False)
```

profile of v0, /device:TPU:8, one launch (start us, length us, event | category | flops | bytes accessed | tf_op | source)
XLA Modules:
  0.0 252.3 jit_solution(14611709308456728059)
XLA Ops:
  7.2 0.0 copy-start
  7.2 0.0 all-gather.2.cloned.1.call-start
  7.2 0.7 all-gather.2.cloned.1.call-update
  7.9 0.0 reduce-scatter.2.cloned.1.call-start
  8.0 0.8 reshape.57
  8.7 0.7 compare_select_fusion
  9.4 0.1 reshape.49
  9.5 0.7 iota_compare_fusion
  10.2 41.6 %all-gather.2.cloned.1.call-done = bf16[8192,128]{1,0:T(8,128)(2,1)} async-done(((bf16[512,128]{1,0:T(8,128)(2,1)}), bf16[8192,128]{1,0:T(8,128)(2,1)}) %all-gather.2.cloned.1.call-update) | async-done | bytes 2097168 | tf_op jit(solution)/shard_map/all_gather | solution.py:13
  51.8 3.9 %gather_fusion = bf16[64,128,128]{2,1,0:T(8,128)(2,1)} fusion(bf16[64,128,128]{2,1,0:T(8,128)(2,1)} %bitcast.23, s32[1024]{0:T(1024)S(1)} %pad_clamp_fusion), kind=kCustom, calls=%fused_computation | custom fusion | bytes 4194560 | tf_op jit(solution)/shard_map/gather | solution.py:15
  55.7 2.4 fusion.1
  58.1 1.4 fusion.5
  59.5 0.4 convolution_convert_fusion
  59.9 2.9 %fusion = f32[4,16,128,128]{3,2,1,0:T(8,128)} fusion(bf16[4,128,128,1]{2,1,3,0:T(8,128)(2,1)S(1)} %bitcast.25, bf16[4,16,128,128]{3,2,1,0:T(8,128)(2,1)S(1)} %copy-done.1, pred[4,16]{1,0:T(4,128)(4,1)S(1)} %iota_compare_fusion), kind=kOutput, calls=%fused_computation.3 | convolution fusion | flops 269484032 | bytes 6422592 | tf_op jit(solution)/shard_map/pbij,pif->pbjf/dot_general | solution.py:27
  62.8 2.5 broadcast_in_dim.23
  65.2 13.6 %scatter_fusion = f32[64,128,128]{2,1,0:T(8,128)} fusion(f32[64,128,128]{2,1,0:T(8,128)} %broadcast_in_dim.23, s32[64]{0:T(128)S(1)} %reshape.57, f32[64,128,128]{2,1,0:T(8,128)} %bitcast.22), kind=kCustom, calls=%fused_computation.1 | custom fusion | flops 1048576 | bytes 12583168 | tf_op jit(solution)/shard_map/scatter-add | solution.py:35
  78.9 0.0 reduce-scatter.2.cloned.1.call-update
  78.9 0.0 all-reduce.2.cloned.1.call-start
  78.9 1.3 fusion.15
  80.2 0.0 all-reduce.2.cloned.1.call-update
  80.2 70.3 %reduce-scatter.2.cloned.1.call-done = f32[512,128]{1,0:T(8,128)} async-done(((f32[8192,128]{1,0:T(8,128)}), f32[512,128]{1,0:T(8,128)}) %reduce-scatter.2.cloned.1.call-update) | async-done | bytes 262160 | tf_op jit(solution)/shard_map/reduce_scatter | solution.py:38
  150.5 1.6 convert_element_type.16
  152.1 92.0 %all-reduce.2.cloned.1.call-done = f32[128,256]{1,0:T(8,128)} async-done(((f32[128,256]{1,0:T(8,128)}), f32[128,256]{1,0:T(8,128)}) %all-reduce.2.cloned.1.call-update) | async-done | bytes 131088 | tf_op jit(solution)/shard_map/psum | solution.py:45
  244.2 1.6 copy.15
  (6 shorter events, 0.0 us)
Async XLA Ops:
  7.2 50.9 %copy-start = (bf16[128,256]{1,0:T(8,128)(2,1)S(1)}, bf16[128,256]{1,0:T(8,128)(2,1)}, u32[]{:S(2)}) copy-start(bf16[128,256]{1,0:T(8,128)(2,1)} %param.7) | copy-start | bytes 196612
  7.2 44.6 %all-gather.2.cloned.1.call-start = ((), (), s32[]{:S(2)}) async-start(), calls=%async_computation.1 | async-start | bytes 2228224 | tf_op jit(solution)/shard_map/all_gather | solution.py:13
  7.9 142.6 %reduce-scatter.2.cloned.1.call-start = ((), (), s32[]{:S(2)}) async-start(), calls=%async_computation.2 | async-start | bytes 4456448 | tf_op jit(solution)/shard_map/reduce_scatter | solution.py:38
  51.8 3.9 %copy-start.1 = (bf16[4,16,128,128]{3,2,1,0:T(8,128)(2,1)S(1)}, bf16[4,16,128,128]{3,2,1,0:T(8,128)(2,1)}, u32[]{:S(2)}) copy-start(bf16[4,16,128,128]{3,2,1,0:T(8,128)(2,1)} %param.10) | copy-start | bytes 6291460
  55.7 2.4 copy-start.2
  78.9 165.3 %all-reduce.2.cloned.1.call-start = ((), (), s32[]{:S(2)}) async-start(), calls=%async_computation.3 | async-start | bytes 262144 | tf_op jit(solution)/shard_map/psum | solution.py:45
Sparse Core Ops, SparseCore 0:
  10.2 41.5 all-gather.1
  79.0 71.4 reduce-scatter.1
  154.9 89.1 all-reduce.1
where the time goes:
time: 253 us; the launch traced here: 252 us
  waiting for transfers between devices  205 us (81%)
  other arithmetic  16.7 us (7%)
  between operations  13.8 us (5%)
  local copies, waits for them, and re-layouts  8.74 us (3%)
  matrix products  8.36 us (3%)
    psum x1, waiting for transfers between devices, body(): weight_grad = lax.psum(partial_value, 'row')  92 us
    reduce_scatter x1, waiting for transfers between devices, body(): lax.psum_scatter(summed.reshape(lax.axis_size('row') * node_rows, in_widt...  70.3 us
    all_gather x1, waiting for transfers between devices, body(): whole = lax.all_gather(features, 'row', axis=0, tiled=True)  41.6 us
    scatter-add x1, other arithmetic, body(): jax.ops.segment_sum(contrib, flat_cols, num_segments=lax.axis_size('row')...  13.6 us
  transfers between devices with their start and end apart: 3, of which 3 were waited for; matrix products, arithmetic and copies ran while one was open for 2% of the time, Pallas kernels for 0%

commit v1 on v0

--- a/solution.py
+++ b/solution.py
@@ -42,7 +42,7 @@
         tiled=True,
     )
     feat_grad = feat_term.astype(jnp.bfloat16)
-    weight_grad = lax.psum(partial_value, "row")
+    weight_grad = lax.all_gather(partial_value, "row").sum(axis=0)
     return (hidden.astype(jnp.bfloat16), feat_grad, weight_grad)
 
 

time: 253 us -> 187 us (0.74)
  waiting for transfers between devices: 205 us -> 137 us
    psum x1 -> x0, waiting for transfers between devices: 92 us -> none  [body(): weight_grad = lax.psum(partial_value, 'row')]
    all_gather x0 -> x1, waiting for transfers between devices: none -> 20.7 us  [body(): weight_grad = lax.all_gather(partial_value, 'row').sum(axis=0)]
    reduce_scatter x1, waiting for transfers between devices: 70.3 us -> 73 us  [body(): lax.psum_scatter(summed.reshape(lax.axis_size('row') * node_rows, in_widt...]
  transfers between devices with their start and end apart: 3 -> 3, of which waited for: 3 -> 3; matrix products, arithmetic and copies ran while one was open for 2% -> 13% of each run, Pallas kernels for 0% -> 0%
where the time goes in v1:
time: 187 us; the launch traced here: 185 us
  waiting for transfers between devices  137 us (73%)
  other arithmetic  19.1 us (10%)
  between operations  13.8 us (7%)
  matrix products  8.4 us (4%)
  local copies, waits for them, and re-layouts  6.49 us (3%)
    reduce_scatter x1, waiting for transfers between devices, body(): lax.psum_scatter(summed.reshape(lax.axis_size('row') * node_rows, in_widt...  73 us
    all_gather x1, waiting for transfers between devices, body(): whole = lax.all_gather(features, 'row', axis=0, tiled=True)  42.3 us
    all_gather x1, waiting for transfers between devices, body(): weight_grad = lax.all_gather(partial_value, 'row').sum(axis=0)  20.7 us
    scatter-add x1, other arithmetic, body(): jax.ops.segment_sum(contrib, flat_cols, num_segments=lax.axis_size('row')...  13.7 us
    gather x1, local copies, waits for them, and re-layouts, body(): picked = whole.reshape(col_blocks, block_side, in_width)[block_cols]  3.85 us
  transfers between devices with their start and end apart: 3, of which 3 were waited for; matrix products, arithmetic and copies ran while one was open for 13% of the time, Pallas kernels for 0%

profile of v1, /device:TPU:8, one launch (start us, length us, event | category | flops | bytes accessed | tf_op | source)
XLA Modules:
  0.0 184.7 jit_solution(185880409076906296)
XLA Ops:
  7.2 0.0 copy-start
  7.2 0.0 all-gather.4.cloned.1.call-start
  7.2 0.7 all-gather.4.cloned.1.call-update
  7.9 0.0 all-gather.6.cloned.1.call-start
  8.0 0.7 compare_select_fusion
  8.6 0.1 reshape.49
  8.7 0.7 iota_compare_fusion
  9.5 42.3 %all-gather.4.cloned.1.call-done = bf16[8192,128]{1,0:T(8,128)(2,1)} async-done(((bf16[512,128]{1,0:T(8,128)(2,1)}), bf16[8192,128]{1,0:T(8,128)(2,1)}) %all-gather.4.cloned.1.call-update) | async-done | bytes 2097168 | tf_op jit(solution)/shard_map/all_gather | solution.py:13
  51.8 3.9 %gather_fusion = bf16[64,128,128]{2,1,0:T(8,128)(2,1)} fusion(bf16[64,128,128]{2,1,0:T(8,128)(2,1)} %bitcast.25, s32[1024]{0:T(1024)S(1)} %pad_clamp_fusion), kind=kCustom, calls=%fused_computation | custom fusion | bytes 4194560 | tf_op jit(solution)/shard_map/gather | solution.py:15
  55.7 2.4 %fusion.1 = f32[4,128,128,1]{2,1,3,0:T(8,128)S(1)} fusion(bf16[4,16,128,128]{3,2,1,0:T(8,128)(2,1)} %bitcast.26, bf16[4,16,128,128]{3,2,1,0:T(8,128)(2,1)S(1)} %copy-done.1, pred[4,16]{1,0:T(4,128)(4,1)S(1)} %iota_compare_fusion), kind=kOutput, calls=%fused_computation.4 | convolution fusion | flops 269484032 | bytes 4456512 | tf_op jit(solution)/shard_map/pbij,pbjf->pif/dot_general | solution.py:16
  58.1 1.4 fusion.5
  59.5 1.3 fusion.15
  60.8 0.0 all-gather.6.cloned.1.call-update
  60.8 0.0 reduce-scatter.2.cloned.1.call-start
  60.9 0.1 reshape.57
  61.0 0.4 convolution_convert_fusion
  61.3 2.9 %fusion = f32[4,16,128,128]{3,2,1,0:T(8,128)} fusion(bf16[4,128,128,1]{2,1,3,0:T(8,128)(2,1)S(1)} %bitcast.27, bf16[4,16,128,128]{3,2,1,0:T(8,128)(2,1)S(1)} %copy-done.1, pred[4,16]{1,0:T(4,128)(4,1)S(1)} %iota_compare_fusion), kind=kOutput, calls=%fused_computation.3 | convolution fusion | flops 269484032 | bytes 6422592 | tf_op jit(solution)/shard_map/pbij,pif->pbjf/dot_general | solution.py:27
  64.3 2.4 %broadcast_in_dim.23 = f32[64,128,128]{2,1,0:T(8,128)} broadcast(f32[]{:T(128)} %constant.8.clone.1), dimensions={} | broadcast | bytes 4194308 | tf_op jit(solution)/shard_map/broadcast_in_dim | solution.py:35
  66.7 13.7 %scatter_fusion = f32[64,128,128]{2,1,0:T(8,128)} fusion(f32[64,128,128]{2,1,0:T(8,128)} %broadcast_in_dim.23, s32[64]{0:T(128)S(1)} %reshape.57, f32[64,128,128]{2,1,0:T(8,128)} %bitcast.23), kind=kCustom, calls=%fused_computation.1 | custom fusion | flops 1048576 | bytes 12583168 | tf_op jit(solution)/shard_map/scatter-add | solution.py:35
  80.4 0.0 reduce-scatter.2.cloned.1.call-update
  80.4 20.7 %all-gather.6.cloned.1.call-done = f32[2048,256]{1,0:T(8,128)} async-done(((f32[128,256]{1,0:T(8,128)}), f32[2048,256]{1,0:T(8,128)}) %all-gather.6.cloned.1.call-update) | async-done | bytes 2097168 | tf_op jit(solution)/shard_map/all_gather | solution.py:45
  101.1 2.4 %reduce_sum.9 = f32[128,256]{1,0:T(8,128)} reduce(f32[16,128,256]{2,1,0:T(8,128)} %bitcast.24, f32[]{:T(128)} %constant.8.clone.1), dimensions={0}, to_apply=%region_2.3 | reduce | flops 491520 | bytes 2228228 | tf_op jit(solution)/shard_map/reduce_sum | solution.py:45
  103.5 73.0 %reduce-scatter.2.cloned.1.call-done = f32[512,128]{1,0:T(8,128)} async-done(((f32[8192,128]{1,0:T(8,128)}), f32[512,128]{1,0:T(8,128)}) %reduce-scatter.2.cloned.1.call-update) | async-done | bytes 262160 | tf_op jit(solution)/shard_map/reduce_scatter | solution.py:38
  176.6 1.6 convert_element_type.16
  (8 shorter events, 0.0 us)
Async XLA Ops:
  7.2 50.9 %copy-start = (bf16[128,256]{1,0:T(8,128)(2,1)S(1)}, bf16[128,256]{1,0:T(8,128)(2,1)}, u32[]{:S(2)}) copy-start(bf16[128,256]{1,0:T(8,128)(2,1)} %param.7) | copy-start | bytes 196612
  7.2 44.6 %all-gather.4.cloned.1.call-start = ((), (), s32[]{:S(2)}) async-start(), calls=%async_computation.1 | async-start | bytes 2228224 | tf_op jit(solution)/shard_map/all_gather | solution.py:13
  7.9 93.2 %all-gather.6.cloned.1.call-start = ((), (), s32[]{:S(2)}) async-start(), calls=%async_computation.3 | async-start | bytes 2228224 | tf_op jit(solution)/shard_map/all_gather | solution.py:45
  51.8 3.9 %copy-start.1 = (bf16[4,16,128,128]{3,2,1,0:T(8,128)(2,1)S(1)}, bf16[4,16,128,128]{3,2,1,0:T(8,128)(2,1)}, u32[]{:S(2)}) copy-start(bf16[4,16,128,128]{3,2,1,0:T(8,128)(2,1)} %param.10) | copy-start | bytes 6291460
  55.7 2.4 %copy-start.3 = (bf16[512,256]{1,0:T(8,128)(2,1)S(1)}, bf16[512,256]{1,0:T(8,128)(2,1)}, u32[]{:S(2)}) copy-start(bf16[512,256]{1,0:T(8,128)(2,1)} %param.11) | copy-start | bytes 786436
  58.1 2.8 %copy-start.2 = (s32[4,16]{1,0:T(4,128)S(1)}, s32[4,16]{1,0:T(4,128)}, u32[]{:S(2)}) copy-start(s32[4,16]{1,0:T(4,128)} %param.8) | copy-start | bytes 772
  60.8 115.7 %reduce-scatter.2.cloned.1.call-start = ((), (), s32[]{:S(2)}) async-start(), calls=%async_computation.2 | async-start | bytes 4456448 | tf_op jit(solution)/shard_map/reduce_scatter | solution.py:38
Sparse Core Ops, SparseCore 0:
  10.2 41.5 all-gather.3
  60.9 40.1 all-gather.5
  105.0 71.5 reduce-scatter.1
